TPU v7x, 32 devices: a whole 2x2x4 slice. The times are simulated.
32 devices in a mesh: exp: 8 (over y, x, core), tp: 4 (over z).
Axes of the slice: x: 2, y: 2, z: 4, core: 2. Of those that a mesh axis runs over, the one named last changes fastest.
Arguments:
- tokens: bfloat16 [65536, 384], P(('exp', 'tp')), may hold values from -24 to 24
- cotangent: bfloat16 [65536, 384], P(('exp', 'tp')), may hold values from -1 to 1
- routes: int32 [65536, 2], P(('exp', 'tp')), may hold values from 0 to 7, all different within a row; in each aligned block of 2048 rows (0 to 2047, 2048 to 4095, ...) at most 1024 rows name the same one
- segments: int32 [64, 1024], P(('exp', 'tp')), may hold values from 0 to 7, never falling along the last dimension, each value on 1 to 256 neighbouring positions
- variates: int32 [64, 1024], P(('exp', 'tp')), may hold values from 0 to 3
- positions: int32 [64, 1024], P(('exp', 'tp')), may hold values from 0 to 1023
- step_count: int32 [1], replicated, may hold values from 1 to 20
- dense_state: float32 [4, 592896], P(None, ('exp', 'tp')), as said below
- gate_up_state: float32 [4, 8, 2, 384, 512], P(None, 'exp', None, None, 'tp'), as said below
- down_state: float32 [4, 8, 512, 384], P(None, 'exp', 'tp'), as said below
- small_state: float32 [4, 780], replicated, as said below
Outputs:
- block_out: bfloat16 [65536, 384], P(('exp', 'tp'))
- grad_in: bfloat16 [65536, 384], P(('exp', 'tp'))
- dense_new: float32 [4, 592896], P(None, ('exp', 'tp'))
- dense_copy: bfloat16 [592896], P(('exp', 'tp'))
- gate_up_new: float32 [4, 8, 2, 384, 512], P(None, 'exp', None, None, 'tp')
- gate_up_copy: bfloat16 [8, 2, 384, 512], P('exp', None, None, 'tp')
- down_new: float32 [4, 8, 512, 384], P(None, 'exp', 'tp')
- down_copy: bfloat16 [8, 512, 384], P('exp', 'tp')
- small_new: float32 [4, 780], replicated
Inputs may be any that keep to these rules, and one draw needn't show every extreme that they name: `routes`: in each aligned block of 2048 rows (the tokens of one device) no expert is named by more than 1024 rows, a bound that some block reaches; the 2 ids of a row differ. `segments`: within a row the ids never fall; a segment has at most a quarter of 1024 tokens. `dense_state`: index 2 is positive. `gate_up_state`: index 2 is positive. `down_state`: index 2 is positive. `small_state`: index 2 is positive.
All inputs are finite; a program needn't handle non-finite values.
Results may differ from a plain program's by a relative error of at most 0.015.
Values may be sent and summed in bfloat16 or wider, within the bound.
No kernel may reach another device: no remote copies, remote signals or barrier semaphores. Data moves between devices by JAX's collectives and lax.ppermute only.
A program may use at most 384 MiB of HBM per device.

v0:
```python
from functools import partial
import math
import jax
import jax.numpy as jnp
from jax import lax
from jax.sharding import PartitionSpec as P

D = 384
HEADS = 6
HD = 64
TOP = 2
SEQ = 1024
norm_epsilon = 1e-06
masked_score = -1e30
moment_rate = 0.5
average_rate = 0.9
adam_epsilon = 1e-08
weight_decay = 0.1
rate_dense = 0.05
rate_expert = 0.04
rate_small = 0.2


def product(left, right):
    return jnp.dot(left, right, preferred_element_type=jnp.float32)


def left_product(left, right):
    return lax.dot_general(
        left, right, (((0,), (0,)), ((), ())), preferred_element_type=jnp.float32
    )


def right_product(left, right):
    return lax.dot_general(
        left, right, (((1,), (1,)), ((), ())), preferred_element_type=jnp.float32
    )


def normalize(values, gain):
    factor = lax.rsqrt(jnp.mean(values * values, axis=-1, keepdims=True) + norm_epsilon)
    return (values * factor * gain, factor)


def normalize_back(values, factor, gain, grad_out):
    weighted = grad_out * gain
    grad_gain = jnp.sum(grad_out * values * factor, axis=0)
    grad_values = factor * weighted - values * (factor * factor * factor) * jnp.mean(
        weighted * values, axis=-1, keepdims=True
    )
    return (grad_values, grad_gain)


def rotation(position_row):
    frequency = jnp.exp(jnp.arange(HD // 2, dtype=jnp.float32) * (-2.0 * math.log(10000.0) / HD))
    angles = position_row.astype(jnp.float32)[:, None] * frequency[None, :]
    return (jnp.cos(angles)[:, None, :], jnp.sin(angles)[:, None, :])


def rotate(values, cosine, sine_part, direction):
    half_dim = HD // 2
    front_half = values[..., :half_dim]
    back_half = values[..., half_dim:]
    return jnp.concatenate(
        [
            front_half * cosine - direction * back_half * sine_part,
            direction * front_half * sine_part + back_half * cosine,
        ],
        axis=-1,
    )


def make_masks(segment_row, variate_row):
    same_var = (variate_row[:, None] == variate_row[None, :])[None]
    allowed = (segment_row[:, None] == segment_row[None, :])[None]
    return (same_var, allowed)


def raw_scores(queries, key_rows, same_var, allowed, score_bias):
    scores = jnp.einsum(
        "qhd,khd->hqk", queries, key_rows, preferred_element_type=jnp.float32
    ) * HD ** (-0.5)
    scores = scores + jnp.where(
        same_var, score_bias[0][:, None, None], score_bias[1][:, None, None]
    )
    return jnp.where(allowed, scores, masked_score)


def attend_forward(score_bias, packed):
    queries, key_rows, values, segment_row, variate_row = packed
    same_var, allowed = make_masks(segment_row, variate_row)
    scores = raw_scores(queries, key_rows, same_var, allowed, score_bias)
    row_max = jnp.max(scores, axis=-1, keepdims=True)
    weights = jnp.exp(scores - row_max)
    row_total = jnp.sum(weights, axis=-1, keepdims=True)
    probs_low = (weights / row_total).astype(jnp.bfloat16)
    mixed_out = jnp.einsum("hqk,khd->qhd", probs_low, values, preferred_element_type=jnp.float32)
    return (mixed_out.astype(jnp.bfloat16), row_max + jnp.log(row_total))


def attend_backward(score_bias, packed):
    queries, key_rows, values, segment_row, variate_row, summary, grad_mixed = packed
    same_var, allowed = make_masks(segment_row, variate_row)
    probs_full = jnp.exp(raw_scores(queries, key_rows, same_var, allowed, score_bias) - summary)
    grad_probs = jnp.einsum("qhd,khd->hqk", grad_mixed, values, preferred_element_type=jnp.float32)
    grad_values = jnp.einsum(
        "hqk,qhd->khd",
        probs_full.astype(jnp.bfloat16),
        grad_mixed,
        preferred_element_type=jnp.float32,
    )
    row_inner = jnp.sum(probs_full * grad_probs, axis=-1, keepdims=True)
    grad_scores = (probs_full * (grad_probs - row_inner)).astype(jnp.bfloat16)
    score_grads = grad_scores.astype(jnp.float32)
    grad_bias = jnp.stack(
        [
            jnp.sum(jnp.where(same_var, score_grads, 0.0), axis=(1, 2)),
            jnp.sum(jnp.where(same_var, 0.0, score_grads), axis=(1, 2)),
        ]
    )
    grad_queries = jnp.einsum(
        "hqk,khd->qhd", grad_scores, key_rows, preferred_element_type=jnp.float32
    ) * HD ** (-0.5)
    grad_keys = jnp.einsum(
        "hqk,qhd->khd", grad_scores, queries, preferred_element_type=jnp.float32
    ) * HD ** (-0.5)
    return (grad_queries, grad_keys, grad_values, grad_bias)


def to_experts(outgoing):
    return lax.all_to_all(outgoing, "exp", split_axis=0, concat_axis=0, tiled=True)


def from_experts(results):
    return lax.all_to_all(results, "exp", split_axis=0, concat_axis=0, tiled=True)


def expert_forward(arrived, gate_up_low, down_low):
    gate_pre = product(arrived, gate_up_low[0, 0])
    up_pre = product(arrived, gate_up_low[0, 1])
    hidden = (jax.nn.silu(gate_pre) * up_pre).astype(jnp.bfloat16)
    results = product(hidden, down_low[0]).astype(jnp.bfloat16)
    return ((arrived, gate_pre, up_pre, hidden), results)


def expert_backward(stored, grad_arrived, gate_up_low, down_low):
    in_rows, gate_pre, up_pre, hidden = stored
    grad_hidden = right_product(grad_arrived, down_low[0])
    sigmoid = jax.nn.sigmoid(gate_pre)
    grad_gate = (grad_hidden * up_pre * sigmoid * (1.0 + gate_pre * (1.0 - sigmoid))).astype(
        jnp.bfloat16
    )
    grad_up = (grad_hidden * gate_pre * sigmoid).astype(jnp.bfloat16)
    grad_gate_up = jnp.stack([left_product(in_rows, grad_gate), left_product(in_rows, grad_up)])[
        None
    ]
    grad_down = left_product(hidden, grad_arrived)[None]
    grad_in_rows = (
        right_product(grad_gate, gate_up_low[0, 0]) + right_product(grad_up, gate_up_low[0, 1])
    ).astype(jnp.bfloat16)
    grad_gate_up, grad_down = (
        lax.psum_scatter(grad_gate_up, "tp", scatter_dimension=3, tiled=True),
        lax.psum_scatter(grad_down, "tp", scatter_dimension=1, tiled=True),
    )
    return (grad_in_rows, grad_gate_up, grad_down)


def adamw_update(old_state, grad_value, rate, decay, step_value):
    moment_one = moment_rate * old_state[1] + (1.0 - moment_rate) * grad_value
    moment_two = moment_rate * old_state[2] + (1.0 - moment_rate) * grad_value * grad_value
    correction = 1.0 - jnp.power(moment_rate, step_value)
    master = old_state[0] - rate * (
        moment_one / correction / (jnp.sqrt(moment_two / correction) + adam_epsilon)
        + decay * old_state[0]
    )
    average = average_rate * old_state[3] + (1.0 - average_rate) * master
    return jnp.stack([master, moment_one, moment_two, average])


def local(
    tokens,
    cotangent,
    routes,
    segments,
    variates,
    positions,
    step_count,
    dense_state,
    gate_up_state,
    down_state,
    small_state,
):
    tok_count = tokens.shape[0]
    seq_count = segments.shape[0]
    experts = lax.axis_size("exp") * gate_up_state.shape[1]
    capacity = 2 * tok_count * TOP // experts
    flat_weights = lax.all_gather(
        dense_state[0].astype(jnp.bfloat16), ("exp", "tp"), axis=0, tiled=True
    )
    in_proj = flat_weights[: 3 * D * D].reshape(D, 3 * D)
    out_proj = flat_weights[3 * D * D : 4 * D * D].reshape(D, D)
    router_weight = flat_weights[4 * D * D :].reshape(D, experts)
    small_params = small_state[0]
    gain_one = small_params[:D]
    gain_two = small_params[D : 2 * D]
    score_bias = small_params[2 * D :].reshape(2, HEADS)
    gate_up_low = gate_up_state[0].astype(jnp.bfloat16)
    down_low = down_state[0].astype(jnp.bfloat16)
    gate_up_low, down_low = (
        lax.all_gather(gate_up_low, "tp", axis=3, tiled=True),
        lax.all_gather(down_low, "tp", axis=1, tiled=True),
    )
    inputs = tokens.astype(jnp.float32)
    normed_one, scale_one = normalize(inputs, gain_one)
    normed_one = normed_one.astype(jnp.bfloat16)
    projected = product(normed_one, in_proj)
    cosine, sine_part = rotation(positions.reshape(-1))
    queries = rotate(projected[:, :D].reshape(tok_count, HEADS, HD), cosine, sine_part, 1.0).astype(
        jnp.bfloat16
    )
    key_rows = rotate(
        projected[:, D : 2 * D].reshape(tok_count, HEADS, HD), cosine, sine_part, 1.0
    ).astype(jnp.bfloat16)
    values = projected[:, 2 * D :].reshape(tok_count, HEADS, HD).astype(jnp.bfloat16)
    seq_queries = queries.reshape(seq_count, SEQ, HEADS, HD)
    seq_keys = key_rows.reshape(seq_count, SEQ, HEADS, HD)
    seq_values = values.reshape(seq_count, SEQ, HEADS, HD)
    mixed_out, summary = lax.map(
        partial(attend_forward, score_bias), (seq_queries, seq_keys, seq_values, segments, variates)
    )
    mixed_out = mixed_out.reshape(tok_count, D)
    middle = inputs + product(mixed_out, out_proj)
    normed_two, scale_two = normalize(middle, gain_two)
    normed_two = normed_two.astype(jnp.bfloat16)
    logits = product(normed_two, router_weight)
    select = routes[:, :, None] == jnp.arange(experts, dtype=jnp.int32)[None, None, :]
    chosen = jnp.sum(jnp.where(select, logits[:, None, :], 0.0), axis=-1)
    gate_probs = jax.nn.softmax(chosen, axis=-1)
    pair_routes = routes.reshape(-1)
    matches = (pair_routes[:, None] == jnp.arange(experts, dtype=jnp.int32)[None, :]).astype(
        jnp.int32
    )
    slot_rank = jnp.sum((jnp.cumsum(matches, axis=0) - matches) * matches, axis=1)
    slot_index = pair_routes * capacity + slot_rank
    source = (
        jnp.zeros((experts * capacity,), jnp.int32)
        .at[slot_index]
        .set(jnp.arange(tok_count * TOP, dtype=jnp.int32))
    )
    filled = jnp.zeros((experts * capacity,), jnp.int32).at[slot_index].set(1) > 0
    outgoing = jnp.where(filled[:, None], normed_two[source // TOP], 0)
    cot_values = cotangent.astype(jnp.float32)
    grad_pairs = (
        (gate_probs[:, :, None] * cot_values[:, None, :])
        .reshape(tok_count * TOP, D)
        .astype(jnp.bfloat16)
    )
    grad_outgoing = jnp.where(filled[:, None], grad_pairs[source], 0)
    arrived = to_experts(outgoing)
    stored, results = expert_forward(arrived, gate_up_low, down_low)
    returned = from_experts(results)
    grad_arrived = to_experts(grad_outgoing)
    grad_rows, grad_gate_up, grad_down = expert_backward(
        stored, grad_arrived, gate_up_low, down_low
    )
    grad_returned = from_experts(grad_rows)
    out_pairs = returned[slot_index].astype(jnp.float32).reshape(tok_count, TOP, D)
    block_out = (middle + jnp.sum(gate_probs[:, :, None] * out_pairs, axis=1)).astype(jnp.bfloat16)
    grad_gate = jnp.sum(cot_values[:, None, :] * out_pairs, axis=-1)
    grad_chosen = gate_probs * (grad_gate - jnp.sum(gate_probs * grad_gate, axis=-1, keepdims=True))
    grad_logits = jnp.sum(jnp.where(select, grad_chosen[:, :, None], 0.0), axis=1).astype(
        jnp.bfloat16
    )
    back_pairs = grad_returned[slot_index].astype(jnp.float32).reshape(tok_count, TOP, D)
    grad_normed_two = right_product(grad_logits, router_weight) + jnp.sum(back_pairs, axis=1)
    grad_router = left_product(normed_two, grad_logits)
    grad_middle, grad_gain_two = normalize_back(middle, scale_two, gain_two, grad_normed_two)
    grad_middle = grad_middle + cot_values
    grad_branch = grad_middle.astype(jnp.bfloat16)
    grad_out_proj = left_product(mixed_out, grad_branch)
    grad_mixed = (
        right_product(grad_branch, out_proj).astype(jnp.bfloat16).reshape(seq_count, SEQ, HEADS, HD)
    )
    grad_queries, grad_keys, grad_values, grad_bias = lax.map(
        partial(attend_backward, score_bias),
        (seq_queries, seq_keys, seq_values, segments, variates, summary, grad_mixed),
    )
    grad_bias = jnp.sum(grad_bias, axis=0)
    grad_queries = rotate(
        grad_queries.reshape(tok_count, HEADS, HD), cosine, sine_part, -1.0
    ).reshape(tok_count, D)
    grad_keys = rotate(grad_keys.reshape(tok_count, HEADS, HD), cosine, sine_part, -1.0).reshape(
        tok_count, D
    )
    grad_projected = jnp.concatenate(
        [grad_queries, grad_keys, grad_values.reshape(tok_count, D)], axis=1
    ).astype(jnp.bfloat16)
    grad_in_proj = left_product(normed_one, grad_projected)
    grad_normed_one = right_product(grad_projected, in_proj)
    grad_inputs, grad_gain_one = normalize_back(inputs, scale_one, gain_one, grad_normed_one)
    grad_in = (grad_middle + grad_inputs).astype(jnp.bfloat16)
    dense_grad = jnp.concatenate(
        [grad_in_proj.reshape(-1), grad_out_proj.reshape(-1), grad_router.reshape(-1)]
    )
    dense_grad = lax.psum_scatter(dense_grad, ("exp", "tp"), scatter_dimension=0, tiled=True)
    small_grad = lax.psum(
        jnp.concatenate([grad_gain_one, grad_gain_two, grad_bias.reshape(-1)]), ("exp", "tp")
    )
    step_value = step_count[0].astype(jnp.float32)
    dense_new = adamw_update(dense_state, dense_grad, rate_dense, weight_decay, step_value)
    gate_up_new = adamw_update(gate_up_state, grad_gate_up, rate_expert, weight_decay, step_value)
    down_new = adamw_update(down_state, grad_down, rate_expert, weight_decay, step_value)
    small_new = adamw_update(small_state, small_grad, rate_small, 0.0, step_value)
    return (
        block_out,
        grad_in,
        dense_new,
        dense_new[0].astype(jnp.bfloat16),
        gate_up_new,
        gate_up_new[0].astype(jnp.bfloat16),
        down_new,
        down_new[0].astype(jnp.bfloat16),
        small_new,
    )


def solution(mesh):
    in_specs = (
        P(("exp", "tp"), None),
        P(("exp", "tp"), None),
        P(("exp", "tp"), None),
        P(("exp", "tp"), None),
        P(("exp", "tp"), None),
        P(("exp", "tp"), None),
        P(),
        P(None, ("exp", "tp")),
        P(None, "exp", None, None, "tp"),
        P(None, "exp", "tp", None),
        P(),
    )
    out_specs = (
        P(("exp", "tp"), None),
        P(("exp", "tp"), None),
        P(None, ("exp", "tp")),
        P(("exp", "tp")),
        P(None, "exp", None, None, "tp"),
        P("exp", None, None, "tp"),
        P(None, "exp", "tp", None),
        P("exp", "tp", None),
        P(),
    )
    return jax.shard_map(local, mesh=mesh, in_specs=in_specs, out_specs=out_specs, check_vma=False)
```

profile of v0, /device:TPU:0, one launch (start us, length us, event | category | flops | bytes accessed | tf_op | source)
XLA Modules:
  0.0 1325.2 jit_solution(2155927653004741738)
XLA Ops:
  19.1 15.5 %scatter_custom_fusion.1 = s32[8192]{0:T(1024)S(1)} fusion(s32[4096]{0:T(1024)S(1)} %bitcast.346, s32[4096]{0:T(1024)S(1)} %iota.21, s32[]{:T(128)} %constant.51.clone.1), kind=kCustom, calls=%fused_computation.210 | custom fusion | bytes 32772 | tf_op jit(solution)/shard_map/scatter | solution.py:248
  34.6 15.8 %scatter_custom_fusion = s32[8192]{0:T(1024)S(1)} fusion(s32[4096]{0:T(1024)S(1)} %bitcast.347, s32[4096]{0:T(1024)S(1)} %broadcast.453, s32[]{:T(128)} %constant.51.clone.1), kind=kCustom, calls=%fused_computation.213 | custom fusion | bytes 32772 | tf_op jit(solution)/shard_map/scatter | solution.py:250
  76.0 70.9 %all-reduce.5.cloned.1.call-done = bf16[592896]{0:T(1024)(128)(2,1)} async-done(((bf16[592896]{0:T(1024)(128)(2,1)}), bf16[592896]{0:T(1024)(128)(2,1)}) %all-reduce.5.cloned.1.call-update) | async-done | bytes 1185808
  182.2 85.0 %while.28 = (s32[]{:T(128)}, bf16[2,1024,6,64]{1,3,2,0:T(8,128)(2,1)}, f32[2,6,1024,1]{2,1,3,0:T(8,128)S(1)}, bf16[2,1024,6,64]{1,3,2,0:T(8,128)(2,1)}, s32[2,10...) while((s32[]{:T(128)}, ...), condition=%wide.region_4.5_spmd, body=%wide.region_1.4_spmd.sunk | while | flops 1726343168 | bytes 106172760 | solution.py:228
  184.1 13.3 %fusion.149 = (f32[6,1024]{1,0:T(8,128)S(1)}, f32[6,1024,1024]{1,2,0:T(8,128)}) fusion(f32[6]{0:T(128)S(1)} %get-tuple-element.555, f32[6]{0:T(128)S(1)} %get-tuple-element.556, pred[1024,1024]{0,1:T(8,128)(4,1)S(1)} %broadcast_compare_fusion.9, pred[1024,1024]{0,1:T(8,128)(4,1)S(1)} %broadcast_compare_fusion.10, ...), kind=kOutput, calls=%fused_computation.10.clone.1 | convolution fusion | flops 836757504 | bytes 28862464 | tf_op jit(solution)/shard_map/while/body/eval_jaxpr/qhd,khd->hqk/dot_general | solution.py:80
  210.0 13.7 %fusion.151 = bf16[2,1024,6,64]{1,3,2,0:T(8,128)(2,1)S(1)} fusion(bf16[2,1024,6,64]{1,3,2,0:T(8,128)(2,1)S(1)} %copy-done.31, s32[]{:T(128)S(6)} %copy.217, f32[6,1024,1024]{1,2,0:T(8,128)} %get-tuple-element.559, f32[6,1024]{1,0:T(8,128)S(1)} %fusion.150, f32[6,1024]{1,0:T(8,128)S(1)} %get-tuple-element.560, f32[6]{0:T(128)S(1)} %get-tuple-element.555, ...), kind=kOutput, calls=%fused_computation.16.clone.1 | convolution fusion | flops 849739776 | bytes 28903424 | tf_op jit(solution)/shard_map/while/body/eval_jaxpr/hqk,khd->qhd/dot_general | solution.py:97
  226.3 13.3 %fusion.149 = (f32[6,1024]{1,0:T(8,128)S(1)}, f32[6,1024,1024]{1,2,0:T(8,128)}) fusion(f32[6]{0:T(128)S(1)} %get-tuple-element.555, f32[6]{0:T(128)S(1)} %get-tuple-element.556, pred[1024,1024]{0,1:T(8,128)(4,1)S(1)} %broadcast_compare_fusion.9, pred[1024,1024]{0,1:T(8,128)(4,1)S(1)} %broadcast_compare_fusion.10, ...), kind=kOutput, calls=%fused_computation.10.clone.1 | convolution fusion | flops 836757504 | bytes 28862464 | tf_op jit(solution)/shard_map/while/body/eval_jaxpr/qhd,khd->hqk/dot_general | solution.py:80
  252.2 13.7 %fusion.151 = bf16[2,1024,6,64]{1,3,2,0:T(8,128)(2,1)S(1)} fusion(bf16[2,1024,6,64]{1,3,2,0:T(8,128)(2,1)S(1)} %copy-done.31, s32[]{:T(128)S(6)} %copy.217, f32[6,1024,1024]{1,2,0:T(8,128)} %get-tuple-element.559, f32[6,1024]{1,0:T(8,128)S(1)} %fusion.150, f32[6,1024]{1,0:T(8,128)S(1)} %get-tuple-element.560, f32[6]{0:T(128)S(1)} %get-tuple-element.555, ...), kind=kOutput, calls=%fused_computation.16.clone.1 | convolution fusion | flops 849739776 | bytes 28903424 | tf_op jit(solution)/shard_map/while/body/eval_jaxpr/hqk,khd->qhd/dot_general | solution.py:97
  284.8 34.8 %gather_fusion.2 = bf16[8192,384]{1,0:T(8,128)(2,1)} fusion(bf16[4096,384]{1,0:T(8,128)(2,1)} %multiply_convert_fusion.4, s32[8192]{0:T(1024)S(1)} %copy-done.59), kind=kCustom, calls=%fused_computation.2 | custom fusion | bytes 12615680 | tf_op jit(solution)/shard_map/gather | solution.py:258
  319.5 33.1 %gather_fusion = bf16[8192,384]{1,0:T(8,128)(2,1)} fusion(bf16[2048,384]{1,0:T(8,128)(2,1)S(1)} %copy.148, s32[8192]{0:T(1024)S(1)} %copy-done.58), kind=kCustom, calls=%fused_computation | custom fusion | bytes 12615680 | tf_op jit(solution)/shard_map/gather | solution.py:251
  361.6 74.9 %all_to_all.42 = bf16[8,1024,384]{2,1,0:T(8,128)(2,1)} all-to-all(bf16[8,1024,384]{2,1,0:T(8,128)(2,1)S(1)} %get-tuple-element.412), channel_id=1, replica_groups=mesh['exp'=8,'tp'=4] {'exp'}, dimensions={0} | all-to-all | bytes 12582912 | tf_op jit(solution)/shard_map/all_to_all | solution.py:131
  442.2 15.1 %all_gather.11 = bf16[1,512,384]{2,1,0:T(8,128)(2,1)S(1)} all-gather(bf16[1,128,384]{2,1,0:T(8,128)(2,1)S(1)} %bitcast_convert_fusion.1), channel_id=1, replica_groups=mesh['exp'=8,'tp'=4] {'tp'}, dimensions={1}, use_global_device_ids=true | all-gather | bytes 491520 | tf_op jit(solution)/shard_map/all_gather | solution.py:211
  458.4 18.0 %all_gather.10 = bf16[1,2,384,512]{3,2,1,0:T(8,128)(2,1)S(1)} all-gather(bf16[1,2,384,128]{3,2,1,0:T(8,128)(2,1)S(1)} %bitcast_convert_fusion), channel_id=1, replica_groups=mesh['exp'=8,'tp'=4] {'tp'}, dimensions={3}, use_global_device_ids=true | all-gather | bytes 983040 | tf_op jit(solution)/shard_map/all_gather | solution.py:210
  496.1 16.8 %all-to-all-done.2 = bf16[8,1024,384]{2,1,0:T(8,128)(2,1)} async-done(((bf16[8,1024,384]{2,1,0:T(8,128)(2,1)}), bf16[8,1024,384]{2,1,0:T(8,128)(2,1)}, u32[]{:S(2)}, u32[]{:S(2)}) %all-to-all-start.2) | async-done | bytes 6291488 | tf_op jit(solution)/shard_map/all_to_all | solution.py:131
  512.9 26.0 %multiply_convert_fusion.1 = (bf16[8192,512]{1,0:T(8,128)(2,1)}, bf16[8192,512]{1,0:T(8,128)(2,1)}, bf16[8192,512]{1,0:T(8,128)(2,1)}) fusion(f32[8192,512]{1,0:T(8,128)} %fusion.69, f32[8192,512]{1,0:T(8,128)} %fusion.70, bf16[8192,384]{1,0:T(8,128)(2,1)} %bitcast.43, bf16[1,512,384]{2,1,0:T(8,128)(2,1)S(1)} %all_gather.11), kind=kOutput, calls=%fused_computation.74 | convolution fusion | flops 3288334336 | bytes 65404928 | tf_op jit(solution)/shard_map/dot_general | solution.py:35
  582.9 50.4 %all-to-all-done.3 = bf16[8,1024,384]{2,1,0:T(8,128)(2,1)} async-done(((bf16[8,1024,384]{2,1,0:T(8,128)(2,1)}), bf16[8,1024,384]{2,1,0:T(8,128)(2,1)}, u32[]{:S(2)}, u32[]{:S(2)}) %all-to-all-start.3) | async-done | bytes 6291488 | tf_op jit(solution)/shard_map/all_to_all | solution.py:135
  659.6 32.7 %reduce-scatter.3.cloned.1.call-done = f32[1,2,384,128]{3,2,1,0:T(8,128)} async-done(((f32[1,2,384,512]{3,2,1,0:T(8,128)}), f32[1,2,384,128]{3,2,1,0:T(8,128)}) %reduce-scatter.3.cloned.1.call-update) | async-done | bytes 393232 | tf_op jit(solution)/shard_map/reduce_scatter | solution.py:162
  695.5 17.6 %gather_fusion.3 = bf16[4096,384]{1,0:T(8,128)(2,1)S(1)} fusion(bf16[8192,384]{1,0:T(8,128)(2,1)} %bitcast.45, s32[4096]{0:T(1024)S(1)} %broadcast_clamp_fusion), kind=kCustom, calls=%fused_computation.3 | custom fusion | bytes 6307840 | tf_op jit(solution)/shard_map/gather | solution.py:274
  717.9 27.3 %reduce_sum.183 = f32[2048,384]{1,0:T(8,128)S(1)} reduce(f32[2048,2,384]{2,1,0:T(2,128)} %reshape.700, f32[]{:T(128)} %constant.55.clone.1), dimensions={1}, to_apply=%region_18.19 | reduce | flops 786432 | bytes 9437188 | tf_op jit(solution)/shard_map/reduce_sum | solution.py:275
  747.7 17.6 %gather_fusion.1 = bf16[4096,384]{1,0:T(8,128)(2,1)S(1)} fusion(bf16[8192,384]{1,0:T(8,128)(2,1)} %bitcast.41, s32[4096]{0:T(1024)S(1)} %broadcast_clamp_fusion), kind=kCustom, calls=%fused_computation.1 | custom fusion | bytes 6307840 | tf_op jit(solution)/shard_map/gather | solution.py:267
  770.0 19.8 %multiply_reduce_fusion.1 = (f32[2048,2]{1,0:T(8,128)}, f32[2048,384]{1,0:T(8,128)}) fusion(f32[2048,2,384]{2,1,0:T(2,128)} %reshape.699, f32[2048,384]{1,0:T(8,128)} %copy.151, f32[2048,2]{1,0:T(8,128)} %copy.144), kind=kLoop, calls=%fused_computation.87 | loop fusion | flops 5500928 | bytes 12615680 | tf_op jit(solution)/shard_map/reduce_sum | solution.py:269
  815.5 290.6 %while.29 = (s32[]{:T(128)}, f32[2,1024,6,64]{1,0,3,2:T(2,128)}, f32[2,1024,6,64]{1,0,3,2:T(2,128)}, bf16[2,1024,6,64]{1,3,2,0:T(8,128)(2,1)}, f32[2,2,6]{2,1,0:...) while((s32[]{:T(128)}, f32[2,1024,6,64]{1,0,3,2:T(2,128)}, ...), condition=%wide.region_24.25_spmd, body=%wide.region_20.24_spmd.sunk | while | flops 4130072576 | bytes 286152160 | solution.py:284
  830.2 20.6 %multiply_reduce_fusion.14 = (f32[6,1024]{1,0:T(8,128)S(1)}, f32[6,1024,1024]{1,2,0:T(8,128)}) fusion(f32[6,1024,1024]{1,2,0:T(8,128)} %fusion.160, f32[6,1024]{1,0:T(8,128)S(1)} %dynamic-slice_bitcast_fusion.2, f32[6]{0:T(128)S(1)} %get-tuple-element.575, f32[6]{0:T(128)S(1)} %get-tuple-element.576, ...), kind=kOutput, calls=%fused_computation.38.clone.1 | convolution fusion | flops 849340416 | bytes 54051888 | tf_op jit(solution)/shard_map/while/body/eval_jaxpr/qhd,khd->hqk/dot_general | solution.py:80
  850.8 23.3 %fusion.161 = (f32[6]{0:T(128)S(1)}, f32[6]{0:T(128)S(1)}, bf16[6,1024,1024]{1,2,0:T(8,128)(2,1)}) fusion(pred[1024,1024]{0,1:T(8,128)(4,1)S(1)} %broadcast_compare_fusion.11, f32[6,1024,1024]{1,2,0:T(8,128)} %get-tuple-element.578, f32[6,1024,1024]{1,2,0:T(8,128)} %fusion.160, f32[6,1024]{1,0:T(8,128)S(1)} %get-tuple-element.579), kind=kLoop, calls=%fused_computation.35.clone.1 | loop fusion | flops 50331632 | bytes 63987760 | tf_op jit(solution)/shard_map/while/body/eval_jaxpr/reduce_sum | solution.py:117
  905.5 27.8 %dynamic_update_slice.37 = f32[2,1024,6,64]{1,0,3,2:T(2,128)} dynamic-update-slice(f32[2,1024,6,64]{1,0,3,2:T(2,128)} %get-tuple-element.630, f32[1,1024,6,64]{1,0,3,2:T(1,128)} %copy.205, s32[]{:T(128)S(6)} %copy.228, s32[]{:T(128)} %constant.51.clone.1..sunk, s32[]{:T(128)} %constant.51.clone.1..sunk, s32[]{:T(128)} %constant.51.clone.1..sunk) | dynamic-update-slice | bytes 3145732 | tf_op jit(solution)/shard_map/while/body/jit(dynamic_update_index_in_dim)/dynamic_update_slice | solution.py:284
  933.3 27.5 %dynamic_update_slice.36 = f32[2,1024,6,64]{1,0,3,2:T(2,128)} dynamic-update-slice(f32[2,1024,6,64]{1,0,3,2:T(2,128)} %get-tuple-element.629, f32[1,1024,6,64]{1,0,3,2:T(1,128)S(1)} %copy-done.1, s32[]{:T(128)S(6)} %copy.228, s32[]{:T(128)} %constant.51.clone.1..sunk, s32[]{:T(128)} %constant.51.clone.1..sunk, s32[]{:T(128)} %constant.51.clone.1..sunk) | dynamic-update-slice | bytes 3145732 | tf_op jit(solution)/shard_map/while/body/jit(dynamic_update_index_in_dim)/dynamic_update_slice | solution.py:284
  975.3 20.6 %multiply_reduce_fusion.14 = (f32[6,1024]{1,0:T(8,128)S(1)}, f32[6,1024,1024]{1,2,0:T(8,128)}) fusion(f32[6,1024,1024]{1,2,0:T(8,128)} %fusion.160, f32[6,1024]{1,0:T(8,128)S(1)} %dynamic-slice_bitcast_fusion.2, f32[6]{0:T(128)S(1)} %get-tuple-element.575, f32[6]{0:T(128)S(1)} %get-tuple-element.576, ...), kind=kOutput, calls=%fused_computation.38.clone.1 | convolution fusion | flops 849340416 | bytes 54051888 | tf_op jit(solution)/shard_map/while/body/eval_jaxpr/qhd,khd->hqk/dot_general | solution.py:80
  995.9 23.3 %fusion.161 = (f32[6]{0:T(128)S(1)}, f32[6]{0:T(128)S(1)}, bf16[6,1024,1024]{1,2,0:T(8,128)(2,1)}) fusion(pred[1024,1024]{0,1:T(8,128)(4,1)S(1)} %broadcast_compare_fusion.11, f32[6,1024,1024]{1,2,0:T(8,128)} %get-tuple-element.578, f32[6,1024,1024]{1,2,0:T(8,128)} %fusion.160, f32[6,1024]{1,0:T(8,128)S(1)} %get-tuple-element.579), kind=kLoop, calls=%fused_computation.35.clone.1 | loop fusion | flops 50331632 | bytes 63987760 | tf_op jit(solution)/shard_map/while/body/eval_jaxpr/reduce_sum | solution.py:117
  1050.6 27.8 %dynamic_update_slice.37 = f32[2,1024,6,64]{1,0,3,2:T(2,128)} dynamic-update-slice(f32[2,1024,6,64]{1,0,3,2:T(2,128)} %get-tuple-element.630, f32[1,1024,6,64]{1,0,3,2:T(1,128)} %copy.205, s32[]{:T(128)S(6)} %copy.228, s32[]{:T(128)} %constant.51.clone.1..sunk, s32[]{:T(128)} %constant.51.clone.1..sunk, s32[]{:T(128)} %constant.51.clone.1..sunk) | dynamic-update-slice | bytes 3145732 | tf_op jit(solution)/shard_map/while/body/jit(dynamic_update_index_in_dim)/dynamic_update_slice | solution.py:284
  1078.4 27.5 %dynamic_update_slice.36 = f32[2,1024,6,64]{1,0,3,2:T(2,128)} dynamic-update-slice(f32[2,1024,6,64]{1,0,3,2:T(2,128)} %get-tuple-element.629, f32[1,1024,6,64]{1,0,3,2:T(1,128)S(1)} %copy-done.1, s32[]{:T(128)S(6)} %copy.228, s32[]{:T(128)} %constant.51.clone.1..sunk, s32[]{:T(128)} %constant.51.clone.1..sunk, s32[]{:T(128)} %constant.51.clone.1..sunk) | dynamic-update-slice | bytes 3145732 | tf_op jit(solution)/shard_map/while/body/jit(dynamic_update_index_in_dim)/dynamic_update_slice | solution.py:284
  1136.9 39.5 %psum.7 = f32[780]{0:T(1024)S(1)} all-reduce(f32[780]{0:T(1024)S(1)} %pad_maximum_fusion.12), channel_id=1, replica_groups=mesh['exp'=8,'tp'=4] {'exp','tp'}, use_global_device_ids=true, to_apply=%region_32.33 | all-reduce | flops 780 | bytes 6240 | tf_op jit(solution)/shard_map/psum | solution.py:306
  1186.8 128.5 %all-reduce.7.cloned.1.call-done = f32[592896]{0:T(1024)} async-done(((f32[592896]{0:T(1024)}), f32[592896]{0:T(1024)}) %all-reduce.7.cloned.1.call-update) | async-done | bytes 2371600
  (378 shorter events, 400.9 us)
Async XLA Ops:
  7.2 139.7 %all-reduce.5.cloned.1.call-start = ((), (), s32[]{:S(2)}) async-start(), calls=%async_computation.8 | async-start | bytes 2371584
  12.9 38.2 %copy-start.28 = (bf16[2048,384]{1,0:T(8,128)(2,1)S(1)}, bf16[2048,384]{1,0:T(8,128)(2,1)}, u32[]{:S(2)}) copy-start(bf16[2048,384]{1,0:T(8,128)(2,1)} %param.15) | copy-start | bytes 4718596
  19.0 31.4 %copy-start.66 = (s32[4096,1]{0,1:T(1,128)}, s32[4096,1]{0,1:T(1,128)S(1)}, u32[]{:S(2)}) copy-start(s32[4096,1]{0,1:T(1,128)S(1)} %compare_select_fusion) | copy-start | bytes 49156
  51.8 97.3 %copy-start.4 = (bf16[2048,384]{0,1:T(8,128)(2,1)}, bf16[2048,384]{0,1:T(8,128)(2,1)S(1)}, u32[]{:S(2)}) copy-start(bf16[2048,384]{0,1:T(8,128)(2,1)S(1)} %copy.139) | copy-start | bytes 4718596
  53.0 96.2 %copy-start.56 = (f32[2048]{0:T(1024)}, f32[2048]{0:T(1024)S(1)}, u32[]{:S(2)}) copy-start(f32[2048]{0:T(1024)S(1)} %get-tuple-element.408) | copy-start | bytes 24580
  74.1 77.8 %copy-start.68 = (f32[384]{0:T(512)}, f32[384]{0:T(512)S(1)}, u32[]{:S(2)}) copy-start(f32[384]{0:T(512)S(1)} %get-tuple-element.305) | copy-start | bytes 4612
  197.4 12.6 copy-start.31
  284.8 34.8 %copy-start.58 = (s32[8192]{0:T(1024)S(1)}, s32[8192]{0:T(1024)}, u32[]{:S(2)}) copy-start(s32[8192]{0:T(1024)} %get-tuple-element.403) | copy-start | bytes 98308
  319.5 33.1 %copy-start.74 = (pred[8,1024]{1,0:T(8,128)(4,1)S(1)}, pred[8,1024]{1,0:T(8,128)(4,1)}, u32[]{:S(2)}) copy-start(pred[8,1024]{1,0:T(8,128)(4,1)} %broadcast_in_dim.212) | copy-start | bytes 24580
  436.5 76.4 %all-to-all-start.2 = ((bf16[8,1024,384]{2,1,0:T(8,128)(2,1)}), bf16[8,1024,384]{2,1,0:T(8,128)(2,1)}, u32[]{:S(2)}, u32[]{:S(2)}) async-start(bf16[8,1024,384]{2,1,0:T(8,128)(2,1)} %get-tuple-element.411), calls=%async_computation.2 | async-start | bytes 12582912 | tf_op jit(solution)/shard_map/all_to_all | solution.py:131
  458.3 29.7 %slice-start = ((s8[6291456]{0:T(1024)(128)(4,1)}), s8[4194304]{0:T(1024)(128)(4,1)S(1)}, s32[]{:S(2)}) async-start(s8[6291456]{0:T(1024)(128)(4,1)} %bitcast.320), calls=%async_computation.10 | async-start | bytes 8388608
  556.9 76.4 %all-to-all-start.3 = ((bf16[8,1024,384]{2,1,0:T(8,128)(2,1)}), bf16[8,1024,384]{2,1,0:T(8,128)(2,1)}, u32[]{:S(2)}, u32[]{:S(2)}) async-start(bf16[8,1024,384]{2,1,0:T(8,128)(2,1)} %bitcast.323), calls=%async_computation.3 | async-start | bytes 12582912 | tf_op jit(solution)/shard_map/all_to_all | solution.py:135
  561.7 95.2 %reduce-scatter.5.cloned.1.call-start = ((), (), s32[]{:S(2)}) async-start(), calls=%async_computation.7 | async-start | bytes 983040 | tf_op jit(solution)/shard_map/reduce_scatter | solution.py:163
  633.3 114.4 %all-to-all-start.1 = ((bf16[8,1024,384]{2,1,0:T(8,128)(2,1)}), bf16[8,1024,384]{2,1,0:T(8,128)(2,1)}, u32[]{:S(2)}, u32[]{:S(2)}) async-start(bf16[8,1024,384]{2,1,0:T(8,128)(2,1)} %bitcast.330), calls=%async_computation.1 | async-start | bytes 12582912 | tf_op jit(solution)/shard_map/all_to_all | solution.py:135
  638.3 53.9 %reduce-scatter.3.cloned.1.call-start = ((), (), s32[]{:S(2)}) async-start(), calls=%async_computation.6 | async-start | bytes 1966080 | tf_op jit(solution)/shard_map/reduce_scatter | solution.py:162
  655.3 37.0 %copy-start.27 = (f32[4,1,2,384,128]{4,3,2,1,0:T(8,128)S(1)}, f32[4,1,2,384,128]{4,3,2,1,0:T(8,128)}, u32[]{:S(2)}) copy-start(f32[4,1,2,384,128]{4,3,2,1,0:T(8,128)} %param.23) | copy-start | bytes 4718596
  655.3 660.0 %all-reduce.7.cloned.1.call-start = ((), (), s32[]{:S(2)}) async-start(), calls=%async_computation.9 | async-start | bytes 4743168
  770.0 21.4 %copy-start.40 = (f32[2048,2]{0,1:T(2,128)S(1)}, f32[2048,2]{0,1:T(2,128)}, u32[]{:S(2)}) copy-start(f32[2048,2]{0,1:T(2,128)} %copy-done.39) | copy-start | bytes 49156
  770.0 21.4 %copy-start.50 = (f32[2048]{0:T(1024)S(1)}, f32[2048]{0:T(1024)}, u32[]{:S(2)}) copy-start(f32[2048]{0:T(1024)} %copy-done.49) | copy-start | bytes 24580
  770.0 21.4 %copy-start.61 = (f32[2048]{0:T(1024)S(1)}, f32[2048]{0:T(1024)}, u32[]{:S(2)}) copy-start(f32[2048]{0:T(1024)} %copy-done.60) | copy-start | bytes 24580
  770.0 21.5 %copy-start.48 = (s32[2048,2]{0,1:T(2,128)S(1)}, s32[2048,2]{0,1:T(2,128)}, u32[]{:S(2)}) copy-start(s32[2048,2]{0,1:T(2,128)} %param.17) | copy-start | bytes 49156
  770.0 24.2 %copy-start.3 = (f32[2048,384]{0,1:T(8,128)S(1)}, f32[2048,384]{0,1:T(8,128)}, u32[]{:S(2)}) copy-start(f32[2048,384]{0,1:T(8,128)} %copy-done.2) | copy-start | bytes 9437188
  770.0 24.1 %copy-start.63 = (f32[2048]{0:T(1024)S(1)}, f32[2048]{0:T(1024)}, u32[]{:S(2)}) copy-start(f32[2048]{0:T(1024)} %copy-done.62) | copy-start | bytes 24580
  770.0 24.1 %copy-start.71 = (f32[384]{0:T(512)S(1)}, f32[384]{0:T(512)}, u32[]{:S(2)}) copy-start(f32[384]{0:T(512)} %get-tuple-element.304) | copy-start | bytes 4612
  850.8 23.3 %copy-start.29 = (bf16[2,1024,6,64]{1,3,2,0:T(8,128)(2,1)S(1)}, bf16[2,1024,6,64]{1,3,2,0:T(8,128)(2,1)}, u32[]{:S(2)}) copy-start(bf16[2,1024,6,64]{1,3,2,0:T(8,128)(2,1)} %get-tuple-element.631) | copy-start | bytes 4718596 | tf_op jit(solution)/shard_map/while
  905.5 27.8 %copy-start.1 = (f32[1,1024,6,64]{1,0,3,2:T(1,128)S(1)}, f32[1,1024,6,64]{1,0,3,2:T(1,128)}, u32[]{:S(2)}) copy-start(f32[1,1024,6,64]{1,0,3,2:T(1,128)} %copy.204) | copy-start | bytes 4718596 | tf_op jit(solution)/shard_map/while
  995.9 23.3 %copy-start.29 = (bf16[2,1024,6,64]{1,3,2,0:T(8,128)(2,1)S(1)}, bf16[2,1024,6,64]{1,3,2,0:T(8,128)(2,1)}, u32[]{:S(2)}) copy-start(bf16[2,1024,6,64]{1,3,2,0:T(8,128)(2,1)} %get-tuple-element.631) | copy-start | bytes 4718596 | tf_op jit(solution)/shard_map/while
  1050.6 27.8 %copy-start.1 = (f32[1,1024,6,64]{1,0,3,2:T(1,128)S(1)}, f32[1,1024,6,64]{1,0,3,2:T(1,128)}, u32[]{:S(2)}) copy-start(f32[1,1024,6,64]{1,0,3,2:T(1,128)} %copy.204) | copy-start | bytes 4718596 | tf_op jit(solution)/shard_map/while
  1184.6 130.7 %copy-start.38 = (f32[18528]{0:T(1024)S(1)}, f32[18528]{0:T(1024)}, u32[]{:S(2)}) copy-start(f32[18528]{0:T(1024)} %copy-done.37) | copy-start | bytes 222340
  1184.6 130.7 %copy-start.44 = (f32[18528]{0:T(1024)S(1)}, f32[18528]{0:T(1024)}, u32[]{:S(2)}) copy-start(f32[18528]{0:T(1024)} %get-tuple-element.296) | copy-start | bytes 222340
  1184.6 130.7 %copy-start.45 = (f32[18528]{0:T(1024)S(1)}, f32[18528]{0:T(1024)}, u32[]{:S(2)}) copy-start(f32[18528]{0:T(1024)} %get-tuple-element.297) | copy-start | bytes 222340
  1184.6 132.4 %copy-start.43 = (f32[18528]{0:T(1024)S(1)}, f32[18528]{0:T(1024)}, u32[]{:S(2)}) copy-start(f32[18528]{0:T(1024)} %get-tuple-element.299) | copy-start | bytes 222340
  (67 other events, 279.4 us)
Sparse Core Ops, SparseCore 0:
  14.0 132.7 all-reduce.4
  572.4 24.7 reduce-scatter.4
  655.4 36.7 reduce-scatter.2
  1180.7 134.5 all-reduce.6
where the time goes:
time: 1340 us; the launch traced here: 1330 us
  local copies, waits for them, and re-layouts  366 us (27%)
  waiting for transfers between devices  299 us (22%)
  matrix products  294 us (22%)
  other arithmetic  186 us (14%)
  blocking collectives  147 us (11%)
  between operations  16.3 us (1%)
  starting transfers between devices  14.7 us (1%)
    unnamed x6, waiting for transfers between devices  199 us
    dynamic_update_slice x8, local copies, waits for them, and re-layouts, local(): lax.map(partial(attend_backward, score_bias), (seq_queries, seq_keys, seq...  122 us
    all_to_all x1, blocking collectives, to_experts(): lax.all_to_all(outgoing, 'exp', split_axis=0, concat_axis=0, tiled=True)  74.9 us
    dot_general x4, matrix products, raw_scores(): jnp.einsum('qhd,khd->hqk', queries, key_rows, preferred_element_type=jnp....  67.9 us
    dot_general x6, matrix products, right_product(): lax.dot_general(left, right, (((1,), (1,)), ((), ())), preferred_element_...  54.4 us
    all_to_all x2, waiting for transfers between devices, from_experts(): lax.all_to_all(results, 'exp', split_axis=0, concat_axis=0, tiled=True)  50.4 us
    reduce_sum x2, other arithmetic, attend_backward(): jnp.sum(jnp.where(same_var, score_grads, 0.0), axis=(1, 2))  46.5 us
    psum x1, blocking collectives, local(): lax.psum(jnp.concatenate([grad_gain_one, grad_gain_two, grad_bias.reshape...  39.5 us
  transfers between devices with their start and end apart: 7, of which 5 were waited for; matrix products, arithmetic and copies ran while one was open for 14% of the time, Pallas kernels for 0%

commit v1 on v0

--- a/solution.py
+++ b/solution.py
@@ -304,7 +304,8 @@
     )
     dense_grad = lax.psum_scatter(dense_grad, ("exp", "tp"), scatter_dimension=0, tiled=True)
     small_grad = lax.psum(
-        jnp.concatenate([grad_gain_one, grad_gain_two, grad_bias.reshape(-1)]), ("exp", "tp")
+        lax.psum(jnp.concatenate([grad_gain_one, grad_gain_two, grad_bias.reshape(-1)]), "tp"),
+        "exp",
     )
     step_value = step_count[0].astype(jnp.float32)
     dense_new = adamw_update(dense_state, dense_grad, rate_dense, weight_decay, step_value)

time: 1340 us -> 1320 us (0.985)
  blocking collectives: 147 us -> 130 us
    psum x1, blocking collectives: 39.5 us -> 9.76 us  [local(): lax.psum(jnp.concatenate([grad_gain_one, grad_gain_two, grad_bias.reshape...]
where the time goes in v1:
time: 1320 us; the launch traced here: 1310 us
  local copies, waits for them, and re-layouts  367 us (28%)
  waiting for transfers between devices  297 us (22%)
  matrix products  294 us (22%)
  other arithmetic  186 us (14%)
  blocking collectives  130 us (10%)
  between operations  16.3 us (1%)
  starting transfers between devices  14.7 us (1%)
    unnamed x6, waiting for transfers between devices  197 us
    dynamic_update_slice x8, local copies, waits for them, and re-layouts, local(): lax.map(partial(attend_backward, score_bias), (seq_queries, seq_keys, seq...  122 us
    all_to_all x1, blocking collectives, to_experts(): lax.all_to_all(outgoing, 'exp', split_axis=0, concat_axis=0, tiled=True)  74.9 us
    dot_general x4, matrix products, raw_scores(): jnp.einsum('qhd,khd->hqk', queries, key_rows, preferred_element_type=jnp....  67.6 us
    dot_general x6, matrix products, right_product(): lax.dot_general(left, right, (((1,), (1,)), ((), ())), preferred_element_...  54.5 us
    all_to_all x2, waiting for transfers between devices, from_experts(): lax.all_to_all(results, 'exp', split_axis=0, concat_axis=0, tiled=True)  50.4 us
    reduce_sum x2, other arithmetic, attend_backward(): jnp.sum(jnp.where(same_var, score_grads, 0.0), axis=(1, 2))  46.5 us
    gather x1, local copies, waits for them, and re-layouts, local(): grad_outgoing = jnp.where(filled[:, None], grad_pairs[source], 0)  34.9 us
  transfers between devices with their start and end apart: 7, of which 5 were waited for; matrix products, arithmetic and copies ran while one was open for 14% of the time, Pallas kernels for 0%

profile of v1, /device:TPU:0, one launch (start us, length us, event | category | flops | bytes accessed | tf_op | source)
XLA Modules:
  0.0 1305.5 jit_solution(1225232878444044)
XLA Ops:
  19.1 15.5 %scatter_custom_fusion.1 = s32[8192]{0:T(1024)S(1)} fusion(s32[4096]{0:T(1024)S(1)} %bitcast.346, s32[4096]{0:T(1024)S(1)} %iota.21, s32[]{:T(128)} %constant.51.clone.1), kind=kCustom, calls=%fused_computation.210 | custom fusion | bytes 32772 | tf_op jit(solution)/shard_map/scatter | solution.py:248
  34.6 15.8 %scatter_custom_fusion = s32[8192]{0:T(1024)S(1)} fusion(s32[4096]{0:T(1024)S(1)} %bitcast.347, s32[4096]{0:T(1024)S(1)} %broadcast.453, s32[]{:T(128)} %constant.51.clone.1), kind=kCustom, calls=%fused_computation.213 | custom fusion | bytes 32772 | tf_op jit(solution)/shard_map/scatter | solution.py:250
  75.9 71.0 %all-reduce.5.cloned.1.call-done = bf16[592896]{0:T(1024)(128)(2,1)} async-done(((bf16[592896]{0:T(1024)(128)(2,1)}), bf16[592896]{0:T(1024)(128)(2,1)}) %all-reduce.5.cloned.1.call-update) | async-done | bytes 1185808
  182.3 84.8 %while.28 = (s32[]{:T(128)}, bf16[2,1024,6,64]{1,3,2,0:T(8,128)(2,1)}, f32[2,6,1024,1]{2,1,3,0:T(8,128)S(1)}, bf16[2,1024,6,64]{1,3,2,0:T(8,128)(2,1)}, s32[2,10...) while((s32[]{:T(128)}, ...), condition=%wide.region_4.5_spmd, body=%wide.region_1.4_spmd.sunk | while | flops 1726343168 | bytes 106172760 | solution.py:228
  184.1 13.3 %fusion.149 = (f32[6,1024]{1,0:T(8,128)S(1)}, f32[6,1024,1024]{1,2,0:T(8,128)}) fusion(f32[6]{0:T(128)S(1)} %get-tuple-element.555, f32[6]{0:T(128)S(1)} %get-tuple-element.556, pred[1024,1024]{0,1:T(8,128)(4,1)S(1)} %broadcast_compare_fusion.9, pred[1024,1024]{0,1:T(8,128)(4,1)S(1)} %broadcast_compare_fusion.10, ...), kind=kOutput, calls=%fused_computation.10.clone.1 | convolution fusion | flops 836757504 | bytes 28862464 | tf_op jit(solution)/shard_map/while/body/eval_jaxpr/qhd,khd->hqk/dot_general | solution.py:80
  210.0 13.7 %fusion.151 = bf16[2,1024,6,64]{1,3,2,0:T(8,128)(2,1)S(1)} fusion(bf16[2,1024,6,64]{1,3,2,0:T(8,128)(2,1)S(1)} %copy-done.31, s32[]{:T(128)S(6)} %copy.217, f32[6,1024,1024]{1,2,0:T(8,128)} %get-tuple-element.559, f32[6,1024]{1,0:T(8,128)S(1)} %fusion.150, f32[6,1024]{1,0:T(8,128)S(1)} %get-tuple-element.560, f32[6]{0:T(128)S(1)} %get-tuple-element.555, ...), kind=kOutput, calls=%fused_computation.16.clone.1 | convolution fusion | flops 849739776 | bytes 28903424 | tf_op jit(solution)/shard_map/while/body/eval_jaxpr/hqk,khd->qhd/dot_general | solution.py:97
  226.2 13.3 %fusion.149 = (f32[6,1024]{1,0:T(8,128)S(1)}, f32[6,1024,1024]{1,2,0:T(8,128)}) fusion(f32[6]{0:T(128)S(1)} %get-tuple-element.555, f32[6]{0:T(128)S(1)} %get-tuple-element.556, pred[1024,1024]{0,1:T(8,128)(4,1)S(1)} %broadcast_compare_fusion.9, pred[1024,1024]{0,1:T(8,128)(4,1)S(1)} %broadcast_compare_fusion.10, ...), kind=kOutput, calls=%fused_computation.10.clone.1 | convolution fusion | flops 836757504 | bytes 28862464 | tf_op jit(solution)/shard_map/while/body/eval_jaxpr/qhd,khd->hqk/dot_general | solution.py:80
  252.1 13.7 %fusion.151 = bf16[2,1024,6,64]{1,3,2,0:T(8,128)(2,1)S(1)} fusion(bf16[2,1024,6,64]{1,3,2,0:T(8,128)(2,1)S(1)} %copy-done.31, s32[]{:T(128)S(6)} %copy.217, f32[6,1024,1024]{1,2,0:T(8,128)} %get-tuple-element.559, f32[6,1024]{1,0:T(8,128)S(1)} %fusion.150, f32[6,1024]{1,0:T(8,128)S(1)} %get-tuple-element.560, f32[6]{0:T(128)S(1)} %get-tuple-element.555, ...), kind=kOutput, calls=%fused_computation.16.clone.1 | convolution fusion | flops 849739776 | bytes 28903424 | tf_op jit(solution)/shard_map/while/body/eval_jaxpr/hqk,khd->qhd/dot_general | solution.py:97
  284.7 34.9 %gather_fusion.2 = bf16[8192,384]{1,0:T(8,128)(2,1)} fusion(bf16[4096,384]{1,0:T(8,128)(2,1)} %multiply_convert_fusion.4, s32[8192]{0:T(1024)S(1)} %copy-done.59), kind=kCustom, calls=%fused_computation.2 | custom fusion | bytes 12615680 | tf_op jit(solution)/shard_map/gather | solution.py:258
  319.6 33.3 %gather_fusion = bf16[8192,384]{1,0:T(8,128)(2,1)} fusion(bf16[2048,384]{1,0:T(8,128)(2,1)S(1)} %copy.148, s32[8192]{0:T(1024)S(1)} %copy-done.58), kind=kCustom, calls=%fused_computation | custom fusion | bytes 12615680 | tf_op jit(solution)/shard_map/gather | solution.py:251
  361.9 74.9 %all_to_all.42 = bf16[8,1024,384]{2,1,0:T(8,128)(2,1)} all-to-all(bf16[8,1024,384]{2,1,0:T(8,128)(2,1)S(1)} %get-tuple-element.412), channel_id=1, replica_groups=mesh['exp'=8,'tp'=4] {'exp'}, dimensions={0} | all-to-all | bytes 12582912 | tf_op jit(solution)/shard_map/all_to_all | solution.py:131
  442.5 15.1 %all_gather.11 = bf16[1,512,384]{2,1,0:T(8,128)(2,1)S(1)} all-gather(bf16[1,128,384]{2,1,0:T(8,128)(2,1)S(1)} %bitcast_convert_fusion.1), channel_id=1, replica_groups=mesh['exp'=8,'tp'=4] {'tp'}, dimensions={1}, use_global_device_ids=true | all-gather | bytes 491520 | tf_op jit(solution)/shard_map/all_gather | solution.py:211
  458.6 18.0 %all_gather.10 = bf16[1,2,384,512]{3,2,1,0:T(8,128)(2,1)S(1)} all-gather(bf16[1,2,384,128]{3,2,1,0:T(8,128)(2,1)S(1)} %bitcast_convert_fusion), channel_id=1, replica_groups=mesh['exp'=8,'tp'=4] {'tp'}, dimensions={3}, use_global_device_ids=true | all-gather | bytes 983040 | tf_op jit(solution)/shard_map/all_gather | solution.py:210
  496.4 16.7 %all-to-all-done.2 = bf16[8,1024,384]{2,1,0:T(8,128)(2,1)} async-done(((bf16[8,1024,384]{2,1,0:T(8,128)(2,1)}), bf16[8,1024,384]{2,1,0:T(8,128)(2,1)}, u32[]{:S(2)}, u32[]{:S(2)}) %all-to-all-start.2) | async-done | bytes 6291488 | tf_op jit(solution)/shard_map/all_to_all | solution.py:131
  513.2 26.0 %multiply_convert_fusion.1 = (bf16[8192,512]{1,0:T(8,128)(2,1)}, bf16[8192,512]{1,0:T(8,128)(2,1)}, bf16[8192,512]{1,0:T(8,128)(2,1)}) fusion(f32[8192,512]{1,0:T(8,128)} %fusion.69, f32[8192,512]{1,0:T(8,128)} %fusion.70, bf16[8192,384]{1,0:T(8,128)(2,1)} %bitcast.43, bf16[1,512,384]{2,1,0:T(8,128)(2,1)S(1)} %all_gather.11), kind=kOutput, calls=%fused_computation.74 | convolution fusion | flops 3288334336 | bytes 65404928 | tf_op jit(solution)/shard_map/dot_general | solution.py:35
  583.2 50.4 %all-to-all-done.3 = bf16[8,1024,384]{2,1,0:T(8,128)(2,1)} async-done(((bf16[8,1024,384]{2,1,0:T(8,128)(2,1)}), bf16[8,1024,384]{2,1,0:T(8,128)(2,1)}, u32[]{:S(2)}, u32[]{:S(2)}) %all-to-all-start.3) | async-done | bytes 6291488 | tf_op jit(solution)/shard_map/all_to_all | solution.py:135
  659.9 32.6 %reduce-scatter.3.cloned.1.call-done = f32[1,2,384,128]{3,2,1,0:T(8,128)} async-done(((f32[1,2,384,512]{3,2,1,0:T(8,128)}), f32[1,2,384,128]{3,2,1,0:T(8,128)}) %reduce-scatter.3.cloned.1.call-update) | async-done | bytes 393232 | tf_op jit(solution)/shard_map/reduce_scatter | solution.py:162
  695.8 17.6 %gather_fusion.3 = bf16[4096,384]{1,0:T(8,128)(2,1)S(1)} fusion(bf16[8192,384]{1,0:T(8,128)(2,1)} %bitcast.45, s32[4096]{0:T(1024)S(1)} %broadcast_clamp_fusion), kind=kCustom, calls=%fused_computation.3 | custom fusion | bytes 6307840 | tf_op jit(solution)/shard_map/gather | solution.py:274
  718.2 27.3 %reduce_sum.183 = f32[2048,384]{1,0:T(8,128)S(1)} reduce(f32[2048,2,384]{2,1,0:T(2,128)} %reshape.700, f32[]{:T(128)} %constant.55.clone.1), dimensions={1}, to_apply=%region_18.19 | reduce | flops 786432 | bytes 9437188 | tf_op jit(solution)/shard_map/reduce_sum | solution.py:275
  748.0 17.6 %gather_fusion.1 = bf16[4096,384]{1,0:T(8,128)(2,1)S(1)} fusion(bf16[8192,384]{1,0:T(8,128)(2,1)} %bitcast.41, s32[4096]{0:T(1024)S(1)} %broadcast_clamp_fusion), kind=kCustom, calls=%fused_computation.1 | custom fusion | bytes 6307840 | tf_op jit(solution)/shard_map/gather | solution.py:267
  770.4 19.8 %multiply_reduce_fusion.1 = (f32[2048,2]{1,0:T(8,128)}, f32[2048,384]{1,0:T(8,128)}) fusion(f32[2048,2,384]{2,1,0:T(2,128)} %reshape.699, f32[2048,384]{1,0:T(8,128)} %copy.151, f32[2048,2]{1,0:T(8,128)} %copy.144), kind=kLoop, calls=%fused_computation.87 | loop fusion | flops 5500928 | bytes 12615680 | tf_op jit(solution)/shard_map/reduce_sum | solution.py:269
  816.0 290.8 %while.29 = (s32[]{:T(128)}, f32[2,1024,6,64]{1,0,3,2:T(2,128)}, f32[2,1024,6,64]{1,0,3,2:T(2,128)}, bf16[2,1024,6,64]{1,3,2,0:T(8,128)(2,1)}, f32[2,2,6]{2,1,0:...) while((s32[]{:T(128)}, f32[2,1024,6,64]{1,0,3,2:T(2,128)}, ...), condition=%wide.region_24.25_spmd, body=%wide.region_20.24_spmd.sunk | while | flops 4130072576 | bytes 286152160 | solution.py:284
  817.5 13.1 %fusion.160 = f32[6,1024,1024]{1,2,0:T(8,128)} fusion(bf16[2,1024,6,64]{1,3,2,0:T(8,128)(2,1)} %get-tuple-element.655, s32[]{:T(128)S(6)} %copy.228, bf16[2,1024,6,64]{1,3,2,0:T(8,128)(2,1)} %get-tuple-element.654), kind=kOutput, calls=%fused_computation.47.clone.1 | convolution fusion | flops 805306368 | bytes 26739712 | tf_op jit(solution)/shard_map/while/body/eval_jaxpr/qhd,khd->hqk/dot_general | solution.py:105
  830.7 20.5 %multiply_reduce_fusion.14 = (f32[6,1024]{1,0:T(8,128)S(1)}, f32[6,1024,1024]{1,2,0:T(8,128)}) fusion(f32[6,1024,1024]{1,2,0:T(8,128)} %fusion.160, f32[6,1024]{1,0:T(8,128)S(1)} %dynamic-slice_bitcast_fusion.2, f32[6]{0:T(128)S(1)} %get-tuple-element.575, f32[6]{0:T(128)S(1)} %get-tuple-element.576, ...), kind=kOutput, calls=%fused_computation.38.clone.1 | convolution fusion | flops 849340416 | bytes 54051888 | tf_op jit(solution)/shard_map/while/body/eval_jaxpr/qhd,khd->hqk/dot_general | solution.py:80
  851.2 23.3 %fusion.161 = (f32[6]{0:T(128)S(1)}, f32[6]{0:T(128)S(1)}, bf16[6,1024,1024]{1,2,0:T(8,128)(2,1)}) fusion(pred[1024,1024]{0,1:T(8,128)(4,1)S(1)} %broadcast_compare_fusion.11, f32[6,1024,1024]{1,2,0:T(8,128)} %get-tuple-element.578, f32[6,1024,1024]{1,2,0:T(8,128)} %fusion.160, f32[6,1024]{1,0:T(8,128)S(1)} %get-tuple-element.579), kind=kLoop, calls=%fused_computation.35.clone.1 | loop fusion | flops 50331632 | bytes 63987760 | tf_op jit(solution)/shard_map/while/body/eval_jaxpr/reduce_sum | solution.py:117
  905.9 27.9 %dynamic_update_slice.37 = f32[2,1024,6,64]{1,0,3,2:T(2,128)} dynamic-update-slice(f32[2,1024,6,64]{1,0,3,2:T(2,128)} %get-tuple-element.630, f32[1,1024,6,64]{1,0,3,2:T(1,128)} %copy.205, s32[]{:T(128)S(6)} %copy.228, s32[]{:T(128)} %constant.51.clone.1..sunk, s32[]{:T(128)} %constant.51.clone.1..sunk, s32[]{:T(128)} %constant.51.clone.1..sunk) | dynamic-update-slice | bytes 3145732 | tf_op jit(solution)/shard_map/while/body/jit(dynamic_update_index_in_dim)/dynamic_update_slice | solution.py:284
  933.8 27.6 %dynamic_update_slice.36 = f32[2,1024,6,64]{1,0,3,2:T(2,128)} dynamic-update-slice(f32[2,1024,6,64]{1,0,3,2:T(2,128)} %get-tuple-element.629, f32[1,1024,6,64]{1,0,3,2:T(1,128)S(1)} %copy-done.1, s32[]{:T(128)S(6)} %copy.228, s32[]{:T(128)} %constant.51.clone.1..sunk, s32[]{:T(128)} %constant.51.clone.1..sunk, s32[]{:T(128)} %constant.51.clone.1..sunk) | dynamic-update-slice | bytes 3145732 | tf_op jit(solution)/shard_map/while/body/jit(dynamic_update_index_in_dim)/dynamic_update_slice | solution.py:284
  975.9 20.5 %multiply_reduce_fusion.14 = (f32[6,1024]{1,0:T(8,128)S(1)}, f32[6,1024,1024]{1,2,0:T(8,128)}) fusion(f32[6,1024,1024]{1,2,0:T(8,128)} %fusion.160, f32[6,1024]{1,0:T(8,128)S(1)} %dynamic-slice_bitcast_fusion.2, f32[6]{0:T(128)S(1)} %get-tuple-element.575, f32[6]{0:T(128)S(1)} %get-tuple-element.576, ...), kind=kOutput, calls=%fused_computation.38.clone.1 | convolution fusion | flops 849340416 | bytes 54051888 | tf_op jit(solution)/shard_map/while/body/eval_jaxpr/qhd,khd->hqk/dot_general | solution.py:80
  996.4 23.3 %fusion.161 = (f32[6]{0:T(128)S(1)}, f32[6]{0:T(128)S(1)}, bf16[6,1024,1024]{1,2,0:T(8,128)(2,1)}) fusion(pred[1024,1024]{0,1:T(8,128)(4,1)S(1)} %broadcast_compare_fusion.11, f32[6,1024,1024]{1,2,0:T(8,128)} %get-tuple-element.578, f32[6,1024,1024]{1,2,0:T(8,128)} %fusion.160, f32[6,1024]{1,0:T(8,128)S(1)} %get-tuple-element.579), kind=kLoop, calls=%fused_computation.35.clone.1 | loop fusion | flops 50331632 | bytes 63987760 | tf_op jit(solution)/shard_map/while/body/eval_jaxpr/reduce_sum | solution.py:117
  1051.1 27.9 %dynamic_update_slice.37 = f32[2,1024,6,64]{1,0,3,2:T(2,128)} dynamic-update-slice(f32[2,1024,6,64]{1,0,3,2:T(2,128)} %get-tuple-element.630, f32[1,1024,6,64]{1,0,3,2:T(1,128)} %copy.205, s32[]{:T(128)S(6)} %copy.228, s32[]{:T(128)} %constant.51.clone.1..sunk, s32[]{:T(128)} %constant.51.clone.1..sunk, s32[]{:T(128)} %constant.51.clone.1..sunk) | dynamic-update-slice | bytes 3145732 | tf_op jit(solution)/shard_map/while/body/jit(dynamic_update_index_in_dim)/dynamic_update_slice | solution.py:284
  1079.0 27.6 %dynamic_update_slice.36 = f32[2,1024,6,64]{1,0,3,2:T(2,128)} dynamic-update-slice(f32[2,1024,6,64]{1,0,3,2:T(2,128)} %get-tuple-element.629, f32[1,1024,6,64]{1,0,3,2:T(1,128)S(1)} %copy-done.1, s32[]{:T(128)S(6)} %copy.228, s32[]{:T(128)} %constant.51.clone.1..sunk, s32[]{:T(128)} %constant.51.clone.1..sunk, s32[]{:T(128)} %constant.51.clone.1..sunk) | dynamic-update-slice | bytes 3145732 | tf_op jit(solution)/shard_map/while/body/jit(dynamic_update_index_in_dim)/dynamic_update_slice | solution.py:284
  1169.6 126.0 %all-reduce.7.cloned.1.call-done = f32[592896]{0:T(1024)} async-done(((f32[592896]{0:T(1024)}), f32[592896]{0:T(1024)}) %all-reduce.7.cloned.1.call-update) | async-done | bytes 2371600
  (379 shorter events, 409.6 us)
Async XLA Ops:
  7.2 139.7 %all-reduce.5.cloned.1.call-start = ((), (), s32[]{:S(2)}) async-start(), calls=%async_computation.8 | async-start | bytes 2371584
  12.9 38.2 %copy-start.28 = (bf16[2048,384]{1,0:T(8,128)(2,1)S(1)}, bf16[2048,384]{1,0:T(8,128)(2,1)}, u32[]{:S(2)}) copy-start(bf16[2048,384]{1,0:T(8,128)(2,1)} %param.15) | copy-start | bytes 4718596
  19.1 31.4 %copy-start.66 = (s32[4096,1]{0,1:T(1,128)}, s32[4096,1]{0,1:T(1,128)S(1)}, u32[]{:S(2)}) copy-start(s32[4096,1]{0,1:T(1,128)S(1)} %compare_select_fusion) | copy-start | bytes 49156
  51.9 97.3 %copy-start.4 = (bf16[2048,384]{0,1:T(8,128)(2,1)}, bf16[2048,384]{0,1:T(8,128)(2,1)S(1)}, u32[]{:S(2)}) copy-start(bf16[2048,384]{0,1:T(8,128)(2,1)S(1)} %copy.139) | copy-start | bytes 4718596
  53.0 96.2 %copy-start.56 = (f32[2048]{0:T(1024)}, f32[2048]{0:T(1024)S(1)}, u32[]{:S(2)}) copy-start(f32[2048]{0:T(1024)S(1)} %get-tuple-element.408) | copy-start | bytes 24580
  74.0 77.9 %copy-start.68 = (f32[384]{0:T(512)}, f32[384]{0:T(512)S(1)}, u32[]{:S(2)}) copy-start(f32[384]{0:T(512)S(1)} %get-tuple-element.305) | copy-start | bytes 4612
  197.4 12.6 copy-start.31
  284.6 34.9 %copy-start.58 = (s32[8192]{0:T(1024)S(1)}, s32[8192]{0:T(1024)}, u32[]{:S(2)}) copy-start(s32[8192]{0:T(1024)} %get-tuple-element.403) | copy-start | bytes 98308
  319.6 33.3 %copy-start.74 = (pred[8,1024]{1,0:T(8,128)(4,1)S(1)}, pred[8,1024]{1,0:T(8,128)(4,1)}, u32[]{:S(2)}) copy-start(pred[8,1024]{1,0:T(8,128)(4,1)} %broadcast_in_dim.212) | copy-start | bytes 24580
  436.8 76.4 %all-to-all-start.2 = ((bf16[8,1024,384]{2,1,0:T(8,128)(2,1)}), bf16[8,1024,384]{2,1,0:T(8,128)(2,1)}, u32[]{:S(2)}, u32[]{:S(2)}) async-start(bf16[8,1024,384]{2,1,0:T(8,128)(2,1)} %get-tuple-element.411), calls=%async_computation.2 | async-start | bytes 12582912 | tf_op jit(solution)/shard_map/all_to_all | solution.py:131
  458.6 29.7 %slice-start = ((s8[6291456]{0:T(1024)(128)(4,1)}), s8[4194304]{0:T(1024)(128)(4,1)S(1)}, s32[]{:S(2)}) async-start(s8[6291456]{0:T(1024)(128)(4,1)} %bitcast.320), calls=%async_computation.10 | async-start | bytes 8388608
  557.2 76.4 %all-to-all-start.3 = ((bf16[8,1024,384]{2,1,0:T(8,128)(2,1)}), bf16[8,1024,384]{2,1,0:T(8,128)(2,1)}, u32[]{:S(2)}, u32[]{:S(2)}) async-start(bf16[8,1024,384]{2,1,0:T(8,128)(2,1)} %bitcast.323), calls=%async_computation.3 | async-start | bytes 12582912 | tf_op jit(solution)/shard_map/all_to_all | solution.py:135
  562.0 95.2 %reduce-scatter.5.cloned.1.call-start = ((), (), s32[]{:S(2)}) async-start(), calls=%async_computation.7 | async-start | bytes 983040 | tf_op jit(solution)/shard_map/reduce_scatter | solution.py:163
  633.6 114.5 %all-to-all-start.1 = ((bf16[8,1024,384]{2,1,0:T(8,128)(2,1)}), bf16[8,1024,384]{2,1,0:T(8,128)(2,1)}, u32[]{:S(2)}, u32[]{:S(2)}) async-start(bf16[8,1024,384]{2,1,0:T(8,128)(2,1)} %bitcast.330), calls=%async_computation.1 | async-start | bytes 12582912 | tf_op jit(solution)/shard_map/all_to_all | solution.py:135
  638.6 53.9 %reduce-scatter.3.cloned.1.call-start = ((), (), s32[]{:S(2)}) async-start(), calls=%async_computation.6 | async-start | bytes 1966080 | tf_op jit(solution)/shard_map/reduce_scatter | solution.py:162
  655.6 37.0 %copy-start.27 = (f32[4,1,2,384,128]{4,3,2,1,0:T(8,128)S(1)}, f32[4,1,2,384,128]{4,3,2,1,0:T(8,128)}, u32[]{:S(2)}) copy-start(f32[4,1,2,384,128]{4,3,2,1,0:T(8,128)} %param.23) | copy-start | bytes 4718596
  655.6 640.1 %all-reduce.7.cloned.1.call-start = ((), (), s32[]{:S(2)}) async-start(), calls=%async_computation.9 | async-start | bytes 4743168
  770.4 21.4 %copy-start.40 = (f32[2048,2]{0,1:T(2,128)S(1)}, f32[2048,2]{0,1:T(2,128)}, u32[]{:S(2)}) copy-start(f32[2048,2]{0,1:T(2,128)} %copy-done.39) | copy-start | bytes 49156
  770.4 21.4 %copy-start.50 = (f32[2048]{0:T(1024)S(1)}, f32[2048]{0:T(1024)}, u32[]{:S(2)}) copy-start(f32[2048]{0:T(1024)} %copy-done.49) | copy-start | bytes 24580
  770.4 21.4 %copy-start.61 = (f32[2048]{0:T(1024)S(1)}, f32[2048]{0:T(1024)}, u32[]{:S(2)}) copy-start(f32[2048]{0:T(1024)} %copy-done.60) | copy-start | bytes 24580
  770.4 21.5 %copy-start.48 = (s32[2048,2]{0,1:T(2,128)S(1)}, s32[2048,2]{0,1:T(2,128)}, u32[]{:S(2)}) copy-start(s32[2048,2]{0,1:T(2,128)} %param.17) | copy-start | bytes 49156
  770.4 24.2 %copy-start.3 = (f32[2048,384]{0,1:T(8,128)S(1)}, f32[2048,384]{0,1:T(8,128)}, u32[]{:S(2)}) copy-start(f32[2048,384]{0,1:T(8,128)} %copy-done.2) | copy-start | bytes 9437188
  770.4 24.2 %copy-start.63 = (f32[2048]{0:T(1024)S(1)}, f32[2048]{0:T(1024)}, u32[]{:S(2)}) copy-start(f32[2048]{0:T(1024)} %copy-done.62) | copy-start | bytes 24580
  770.4 24.1 %copy-start.71 = (f32[384]{0:T(512)S(1)}, f32[384]{0:T(512)}, u32[]{:S(2)}) copy-start(f32[384]{0:T(512)} %get-tuple-element.304) | copy-start | bytes 4612
  851.2 23.3 %copy-start.29 = (bf16[2,1024,6,64]{1,3,2,0:T(8,128)(2,1)S(1)}, bf16[2,1024,6,64]{1,3,2,0:T(8,128)(2,1)}, u32[]{:S(2)}) copy-start(bf16[2,1024,6,64]{1,3,2,0:T(8,128)(2,1)} %get-tuple-element.631) | copy-start | bytes 4718596 | tf_op jit(solution)/shard_map/while
  905.9 27.9 %copy-start.1 = (f32[1,1024,6,64]{1,0,3,2:T(1,128)S(1)}, f32[1,1024,6,64]{1,0,3,2:T(1,128)}, u32[]{:S(2)}) copy-start(f32[1,1024,6,64]{1,0,3,2:T(1,128)} %copy.204) | copy-start | bytes 4718596 | tf_op jit(solution)/shard_map/while
  996.4 23.3 %copy-start.29 = (bf16[2,1024,6,64]{1,3,2,0:T(8,128)(2,1)S(1)}, bf16[2,1024,6,64]{1,3,2,0:T(8,128)(2,1)}, u32[]{:S(2)}) copy-start(bf16[2,1024,6,64]{1,3,2,0:T(8,128)(2,1)} %get-tuple-element.631) | copy-start | bytes 4718596 | tf_op jit(solution)/shard_map/while
  1051.1 27.9 %copy-start.1 = (f32[1,1024,6,64]{1,0,3,2:T(1,128)S(1)}, f32[1,1024,6,64]{1,0,3,2:T(1,128)}, u32[]{:S(2)}) copy-start(f32[1,1024,6,64]{1,0,3,2:T(1,128)} %copy.204) | copy-start | bytes 4718596 | tf_op jit(solution)/shard_map/while
  1167.4 128.3 %copy-start.38 = (f32[18528]{0:T(1024)S(1)}, f32[18528]{0:T(1024)}, u32[]{:S(2)}) copy-start(f32[18528]{0:T(1024)} %copy-done.37) | copy-start | bytes 222340
  1167.4 128.3 %copy-start.44 = (f32[18528]{0:T(1024)S(1)}, f32[18528]{0:T(1024)}, u32[]{:S(2)}) copy-start(f32[18528]{0:T(1024)} %get-tuple-element.296) | copy-start | bytes 222340
  1167.4 128.2 %copy-start.45 = (f32[18528]{0:T(1024)S(1)}, f32[18528]{0:T(1024)}, u32[]{:S(2)}) copy-start(f32[18528]{0:T(1024)} %get-tuple-element.297) | copy-start | bytes 222340
  1167.4 129.9 %copy-start.43 = (f32[18528]{0:T(1024)S(1)}, f32[18528]{0:T(1024)}, u32[]{:S(2)}) copy-start(f32[18528]{0:T(1024)} %get-tuple-element.299) | copy-start | bytes 222340
  (67 other events, 279.5 us)
Sparse Core Ops, SparseCore 0:
  14.0 132.8 all-reduce.4
  572.7 24.7 reduce-scatter.4
  655.7 36.7 reduce-scatter.2
  1163.5 132.1 all-reduce.6
